TPU v7x, 32 devices: a whole 2x2x4 slice. The times are simulated.
32 devices in a mesh: dp: 8 (over y, x, core), mp: 4 (over z).
Axes of the slice: x: 2, y: 2, z: 4, core: 2. Of those that a mesh axis runs over, the one named last changes fastest.
Arguments:
- tokens: bfloat16 [8, 2048, 768], P('dp', 'mp'), may hold values from -6 to 6
- gain_first: float32 [768], replicated, may hold values from 0.5 to 1.5
- input_weight: bfloat16 [768, 3, 768], P(None, None, 'mp'), may hold values from -0.21875 to 0.21875
- kernel: float32 [768, 2048], P('mp'), may hold values from -0.25 to 0.25
- pad_len: int32 [768], P('mp'), may hold values from 0 to 1023
- output_weight: bfloat16 [768, 768], P('mp'), may hold values from -0.21875 to 0.21875
- gain_second: float32 [768], replicated, may hold values from 0.5 to 1.5
- up_weight: bfloat16 [768, 3072], P(None, 'mp'), may hold values from -0.21875 to 0.21875
- down_weight: bfloat16 [3072, 768], P('mp'), may hold values from -0.109375 to 0.109375
- cotangent: bfloat16 [8, 2048, 768], P('dp', 'mp'), may hold values from -6 to 6
Outputs:
- block_out: bfloat16 [8, 2048, 768], P('dp', 'mp')
- grad_tokens: float32 [8, 2048, 768], P('dp', 'mp')
- grad_gain_first: float32 [768], replicated
- grad_w_in: float32 [768, 3, 768], P(None, None, 'mp')
- grad_kernel: float32 [768, 2048], P('mp')
- grad_w_out: float32 [768, 768], P('mp')
- grad_gain_second: float32 [768], replicated
- grad_w_up: float32 [768, 3072], P(None, 'mp')
- grad_w_down: float32 [3072, 768], P('mp')
All inputs are finite; a program needn't handle non-finite values.
Results may differ from a plain program's by a relative error of at most 0.008.
Values may be sent and summed in bfloat16 or wider, within the bound.
No kernel may reach another device: no remote copies, remote signals or barrier semaphores. Data moves between devices by JAX's collectives and lax.ppermute only.
A program may use at most 640 MiB of HBM per device.

v0:
```python
from functools import partial

import jax
import jax.numpy as jnp
from jax import lax
from jax.sharding import PartitionSpec as P

thresh = 0.003
epsilon = 1e-05


def layer_norm(values, scale_vec):
    centered = values - jnp.mean(values, axis=-1, keepdims=True)
    spread = jnp.mean(centered * centered, axis=-1, keepdims=True)
    return centered * lax.rsqrt(spread + epsilon) * scale_vec


def gelu_tanh(values):
    return jax.nn.gelu(values, approximate=True)


def shrink_pool(kernel, pad_len):
    shrunk = jax.nn.relu(kernel - thresh) - jax.nn.relu(-kernel - thresh)
    padded = jnp.pad(shrunk, ((0, 0), (1, 1)))
    pooled = (padded[:, :-2] + padded[:, 1:-1] + padded[:, 2:]) / 3.0
    positions = lax.broadcasted_iota(jnp.int32, pooled.shape, 1)
    return jnp.where(positions < (pooled.shape[1] - pad_len)[:, None], pooled, 0.0)


def causal_conv(mixed_in, filt):
    seq_count, length, channels = mixed_in.shape
    kernel_len = filt.shape[1]
    block_width = min(128, kernel_len)
    block_count = length // block_width
    blocks = mixed_in.reshape(seq_count, block_count, block_width, channels)
    padded = jnp.pad(filt, ((0, 0), (block_width, block_width)))
    offset = (
        lax.broadcasted_iota(jnp.int32, (block_width, block_width), 0)
        - lax.broadcasted_iota(jnp.int32, (block_width, block_width), 1)
        + block_width
    )
    summed = jnp.zeros_like(blocks)
    for lag_index in range(min(kernel_len // block_width + 1, block_count)):
        toeplitz = jnp.take(padded, offset + lag_index * block_width, axis=1)
        shifted = jnp.pad(
            blocks[:, : block_count - lag_index], ((0, 0), (lag_index, 0), (0, 0), (0, 0))
        )
        summed = summed + jnp.einsum(
            "snbc,crb->snrc", shifted, toeplitz, precision=lax.Precision.HIGHEST
        )
    return summed.reshape(seq_count, length, channels)


def mixer(projected_input, kernel, pad_len):
    filt = shrink_pool(kernel, pad_len)
    conv = causal_conv(projected_input[:, :, 1] * projected_input[:, :, 0], filt)
    return projected_input[:, :, 2] * conv


def body(
    tokens,
    gain_first,
    input_weight,
    kernel,
    pad_len,
    output_weight,
    gain_second,
    up_weight,
    down_weight,
    cotangent,
):
    start_rows = tokens.astype(jnp.float32)
    normed_one, first_back = jax.vjp(layer_norm, start_rows, gain_first)
    normed_low = normed_one.astype(jnp.bfloat16)
    normalized_complete = lax.all_gather(normed_low, "mp", axis=1, tiled=True)
    projected_input = jnp.einsum(
        "rqu,uwm->rqwm", normalized_complete, input_weight, preferred_element_type=jnp.float32
    )
    mixer_out, mixer_back = jax.vjp(partial(mixer, pad_len=pad_len), projected_input, kernel)
    mixer_lowrank = mixer_out.astype(jnp.bfloat16)
    partial_output_rows = jnp.einsum(
        "hvw,wm->hvm", mixer_lowrank, output_weight, preferred_element_type=jnp.float32
    )
    mixer_sum = lax.psum_scatter(partial_output_rows, "mp", scatter_dimension=1, tiled=True)
    residual_one = start_rows + mixer_sum
    normed_two, second_back = jax.vjp(layer_norm, residual_one, gain_second)
    second_low = normed_two.astype(jnp.bfloat16)
    second_gate_complete, gradient_complete = (
        lax.all_gather(second_low, "mp", axis=1, tiled=True),
        lax.all_gather(cotangent, "mp", axis=1, tiled=True),
    )
    hidden_preactivation = jnp.einsum(
        "gta,az->gtz", second_gate_complete, up_weight, preferred_element_type=jnp.float32
    )
    hidden_act, act_back = jax.vjp(gelu_tanh, hidden_preactivation)
    activation_lowrank = hidden_act.astype(jnp.bfloat16)
    down_projection_terms = jnp.einsum(
        "ycg,gi->yci", activation_lowrank, down_weight, preferred_element_type=jnp.float32
    )
    block_out = residual_one + lax.psum_scatter(
        down_projection_terms, "mp", scatter_dimension=1, tiled=True
    )
    activation_gradient = jnp.einsum(
        "war,nr->wan", gradient_complete, down_weight, preferred_element_type=jnp.float32
    )
    preactivation_gradient = act_back(activation_gradient)[0].astype(jnp.bfloat16)
    norm_statistic_terms = jnp.einsum(
        "kyu,qu->kyq", preactivation_gradient, up_weight, preferred_element_type=jnp.float32
    )
    grad_norm_two = lax.psum_scatter(norm_statistic_terms, "mp", scatter_dimension=1, tiled=True)
    up_projection_gradient = jnp.einsum(
        "mxz,mxi->zi",
        second_gate_complete,
        preactivation_gradient,
        preferred_element_type=jnp.float32,
    )
    down_projection_gradient = jnp.einsum(
        "jbq,jbx->qx", activation_lowrank, gradient_complete, preferred_element_type=jnp.float32
    )
    grad_mid_norm, gain_second_grad = second_back(grad_norm_two)
    grad_mid = cotangent.astype(jnp.float32) + grad_mid_norm
    grad_mid_low = grad_mid.astype(jnp.bfloat16)
    middle_gradient_complete = lax.all_gather(grad_mid_low, "mp", axis=1, tiled=True)
    w_out_grad = jnp.einsum(
        "eht,ehf->tf", mixer_lowrank, middle_gradient_complete, preferred_element_type=jnp.float32
    )
    mixer_gradient = jnp.einsum(
        "tju,hu->tjh", middle_gradient_complete, output_weight, preferred_element_type=jnp.float32
    )
    grad_proj, kernel_grad = mixer_back(mixer_gradient)
    projection_gradient_lowrank = grad_proj.astype(jnp.bfloat16)
    w_in_grad = jnp.einsum(
        "fgh,fgyv->hyv",
        normalized_complete,
        projection_gradient_lowrank,
        preferred_element_type=jnp.float32,
    )
    first_terms = jnp.einsum(
        "jmwi,rwi->jmr",
        projection_gradient_lowrank,
        input_weight,
        preferred_element_type=jnp.float32,
    )
    grad_norm_one = lax.psum_scatter(first_terms, "mp", scatter_dimension=1, tiled=True)
    grad_start, gain_first_grad = first_back(grad_norm_one)
    grad_tokens = grad_mid + grad_start
    weight_sums = lax.psum(
        (w_in_grad, kernel_grad, w_out_grad, up_projection_gradient, down_projection_gradient), "dp"
    )
    gain_sums = lax.psum((gain_first_grad, gain_second_grad), ("dp", "mp"))
    return (
        block_out.astype(jnp.bfloat16),
        grad_tokens,
        gain_sums[0],
        weight_sums[0],
        weight_sums[1],
        weight_sums[2],
        gain_sums[1],
        weight_sums[3],
        weight_sums[4],
    )


def solution(mesh):
    in_specs = (
        P("dp", "mp", None),
        P(),
        P(None, None, "mp"),
        P("mp", None),
        P("mp"),
        P("mp", None),
        P(),
        P(None, "mp"),
        P("mp", None),
        P("dp", "mp", None),
    )
    out_specs = (
        P("dp", "mp", None),
        P("dp", "mp", None),
        P(),
        P(None, None, "mp"),
        P("mp", None),
        P("mp", None),
        P(),
        P(None, "mp"),
        P("mp", None),
    )
    return jax.shard_map(body, mesh=mesh, in_specs=in_specs, out_specs=out_specs, check_vma=False)
```

profile of v0, /device:TPU:0, one launch (start us, length us, event | category | flops | bytes accessed | tf_op | source)
XLA Modules:
  0.0 4946.7 jit_solution(800908167026821165)
XLA Ops:
  19.7 66.9 %gather_fusion.15 = f32[16384,192]{1,0:T(8,128)} fusion(f32[192,2304]{0,1:T(8,128)S(1)} %pad.217, s32[16384]{0:T(1024)} %broadcast_clamp_fusion), kind=kCustom, calls=%fused_computation.15.clone | custom fusion | bytes 25231360 | tf_op jit(solution)/shard_map/jvp(jit(_take))/gather | solution.py:44
  103.4 66.9 %gather_fusion.14 = f32[16384,192]{1,0:T(8,128)} fusion(f32[192,2304]{0,1:T(8,128)S(1)} %pad.217, s32[16384]{0:T(1024)} %broadcast_clamp_fusion.1), kind=kCustom, calls=%fused_computation.14.clone | custom fusion | bytes 25231360 | tf_op jit(solution)/shard_map/jvp(jit(_take))/gather | solution.py:44
  187.1 66.9 %gather_fusion.13 = f32[16384,192]{1,0:T(8,128)} fusion(f32[192,2304]{0,1:T(8,128)S(1)} %pad.217, s32[16384]{0:T(1024)} %broadcast_clamp_fusion.2), kind=kCustom, calls=%fused_computation.13.clone | custom fusion | bytes 25231360 | tf_op jit(solution)/shard_map/jvp(jit(_take))/gather | solution.py:44
  271.4 66.9 %gather_fusion.12 = f32[16384,192]{1,0:T(8,128)} fusion(f32[192,2304]{0,1:T(8,128)S(1)} %pad.217, s32[16384]{0:T(1024)} %broadcast_clamp_fusion.3), kind=kCustom, calls=%fused_computation.12.clone | custom fusion | bytes 25231360 | tf_op jit(solution)/shard_map/jvp(jit(_take))/gather | solution.py:44
  440.0 66.9 %gather_fusion.10 = f32[16384,192]{1,0:T(8,128)} fusion(f32[192,2304]{0,1:T(8,128)S(1)} %pad.217, s32[16384]{0:T(1024)} %broadcast_clamp_fusion.5), kind=kCustom, calls=%fused_computation.10.clone | custom fusion | bytes 25231360 | tf_op jit(solution)/shard_map/jvp(jit(_take))/gather | solution.py:44
  524.4 66.9 %gather_fusion.9 = f32[16384,192]{1,0:T(8,128)} fusion(f32[192,2304]{0,1:T(8,128)S(1)} %pad.217, s32[16384]{0:T(1024)} %broadcast_clamp_fusion.6), kind=kCustom, calls=%fused_computation.9.clone | custom fusion | bytes 25231360 | tf_op jit(solution)/shard_map/jvp(jit(_take))/gather | solution.py:44
  608.7 66.9 %gather_fusion.8 = f32[16384,192]{1,0:T(8,128)} fusion(f32[192,2304]{0,1:T(8,128)S(1)} %pad.217, s32[16384]{0:T(1024)} %broadcast_clamp_fusion.7), kind=kCustom, calls=%fused_computation.8.clone | custom fusion | bytes 25231360 | tf_op jit(solution)/shard_map/jvp(jit(_take))/gather | solution.py:44
  777.3 66.9 %gather_fusion.6 = f32[16384,192]{1,0:T(8,128)} fusion(f32[192,2304]{0,1:T(8,128)S(1)} %pad.217, s32[16384]{0:T(1024)} %broadcast_clamp_fusion.9), kind=kCustom, calls=%fused_computation.6.clone | custom fusion | bytes 25231360 | tf_op jit(solution)/shard_map/jvp(jit(_take))/gather | solution.py:44
  861.7 66.9 %gather_fusion.5 = f32[16384,192]{1,0:T(8,128)} fusion(f32[192,2304]{0,1:T(8,128)S(1)} %pad.217, s32[16384]{0:T(1024)} %broadcast_clamp_fusion.10), kind=kCustom, calls=%fused_computation.5.clone | custom fusion | bytes 25231360 | tf_op jit(solution)/shard_map/jvp(jit(_take))/gather | solution.py:44
  1114.6 66.9 %gather_fusion.2 = f32[16384,192]{1,0:T(8,128)} fusion(f32[192,2304]{0,1:T(8,128)S(1)} %pad.217, s32[16384]{0:T(1024)} %broadcast_clamp_fusion.13), kind=kCustom, calls=%fused_computation.2.clone | custom fusion | bytes 25231360 | tf_op jit(solution)/shard_map/jvp(jit(_take))/gather | solution.py:44
  1283.7 66.9 %gather_fusion = f32[16384,192]{1,0:T(8,128)} fusion(f32[192,2304]{0,1:T(8,128)S(1)} %pad.217, s32[16384]{0:T(1024)} %broadcast_clamp_fusion.15), kind=kCustom, calls=%fused_computation.clone | custom fusion | bytes 25231360 | tf_op jit(solution)/shard_map/jvp(jit(_take))/gather | solution.py:44
  1742.8 113.6 %reduce-scatter.5.cloned.1.call-done = f32[1,512,768]{2,1,0:T(8,128)} async-done(((f32[1,2048,768]{2,1,0:T(8,128)}), f32[1,512,768]{2,1,0:T(8,128)}) %reduce-scatter.5.cloned.1.call-update) | async-done | bytes 1572880 | tf_op jit(solution)/shard_map/reduce_scatter | solution.py:84
  2014.7 97.7 %reduce-scatter.9.cloned.1.call-done = f32[1,512,768]{2,1,0:T(8,128)} async-done(((f32[1,2048,768]{2,1,0:T(8,128)}), f32[1,512,768]{2,1,0:T(8,128)}) %reduce-scatter.9.cloned.1.call-update) | async-done | bytes 1572880 | tf_op jit(solution)/shard_map/reduce_scatter | solution.py:110
  2115.4 110.4 %reduce-scatter.7.cloned.1.call-done = f32[1,512,768]{2,1,0:T(8,128)} async-done(((f32[1,2048,768]{2,1,0:T(8,128)}), f32[1,512,768]{2,1,0:T(8,128)}) %reduce-scatter.7.cloned.1.call-update) | async-done | bytes 1572880 | tf_op jit(solution)/shard_map/reduce_scatter | solution.py:100
  3166.0 89.6 %scatter_custom_fusion.15 = f32[192,2304]{0,1:T(8,128)} fusion(s32[16384]{0:T(1024)} %fusion.396, f32[16384,192]{1,0:T(8,128)} %bitcast.784, f32[]{:T(128)} %constant.124.clone.1), kind=kCustom, calls=%fused_computation.391 | custom fusion | flops 3145728 | bytes 1769984 | tf_op jit(solution)/shard_map/transpose(jvp(jit(_take)))/scatter-add | solution.py:44
  3255.6 89.8 %scatter_custom_fusion = f32[192,2304]{0,1:T(8,128)} fusion(s32[16384]{0:T(1024)} %fusion.441, f32[16384,192]{1,0:T(8,128)} %bitcast.783, f32[]{:T(128)} %constant.124.clone.1), kind=kCustom, calls=%fused_computation.407 | custom fusion | flops 3145728 | bytes 1769984 | tf_op jit(solution)/shard_map/transpose(jvp(jit(_take)))/scatter-add | solution.py:44
  3345.4 89.7 %scatter_custom_fusion.1 = f32[192,2304]{0,1:T(8,128)} fusion(s32[16384]{0:T(1024)} %fusion.438, f32[16384,192]{1,0:T(8,128)} %bitcast.782, f32[]{:T(128)} %constant.124.clone.1), kind=kCustom, calls=%fused_computation.405 | custom fusion | flops 3145728 | bytes 1769984 | tf_op jit(solution)/shard_map/transpose(jvp(jit(_take)))/scatter-add | solution.py:44
  3437.8 89.6 %scatter_custom_fusion.3 = f32[192,2304]{0,1:T(8,128)} fusion(s32[16384]{0:T(1024)} %fusion.432, f32[16384,192]{1,0:T(8,128)} %bitcast.781, f32[]{:T(128)} %constant.124.clone.1), kind=kCustom, calls=%fused_computation.403 | custom fusion | flops 3145728 | bytes 1769984 | tf_op jit(solution)/shard_map/transpose(jvp(jit(_take)))/scatter-add | solution.py:44
  3527.5 89.0 %scatter_fusion = f32[192,2304]{0,1:T(8,128)S(1)} fusion(f32[192,2304]{0,1:T(8,128)S(1)} %add_any.142, s32[16384]{0:T(1024)S(1)} %copy-done.54, f32[16384,192]{1,0:T(8,128)} %bitcast.751), kind=kCustom, calls=%fused_computation.18 | custom fusion | flops 3145728 | bytes 37814272 | tf_op jit(solution)/shard_map/transpose(jvp(jit(_take)))/scatter-add | solution.py:44
  3619.9 90.1 %scatter_custom_fusion.5 = f32[192,2304]{0,1:T(8,128)} fusion(s32[16384]{0:T(1024)} %fusion.426, f32[16384,192]{1,0:T(8,128)} %bitcast.780, f32[]{:T(128)} %constant.124.clone.1), kind=kCustom, calls=%fused_computation.401 | custom fusion | flops 3145728 | bytes 1769984 | tf_op jit(solution)/shard_map/transpose(jvp(jit(_take)))/scatter-add | solution.py:44
  3709.9 89.0 %scatter_fusion.1 = f32[192,2304]{0,1:T(8,128)S(1)} fusion(f32[192,2304]{0,1:T(8,128)S(1)} %copy-done.2, s32[16384]{0:T(1024)S(1)} %copy-done.53, f32[16384,192]{1,0:T(8,128)} %bitcast.750), kind=kCustom, calls=%fused_computation.20 | custom fusion | flops 3145728 | bytes 37814272 | tf_op jit(solution)/shard_map/transpose(jvp(jit(_take)))/scatter-add | solution.py:44
  3802.3 89.8 %scatter_custom_fusion.7 = f32[192,2304]{0,1:T(8,128)} fusion(s32[16384]{0:T(1024)} %fusion.420, f32[16384,192]{1,0:T(8,128)} %bitcast.779, f32[]{:T(128)} %constant.124.clone.1), kind=kCustom, calls=%fused_computation.399 | custom fusion | flops 3145728 | bytes 1769984 | tf_op jit(solution)/shard_map/transpose(jvp(jit(_take)))/scatter-add | solution.py:44
  3892.1 89.0 %scatter_fusion.2 = f32[192,2304]{0,1:T(8,128)S(1)} fusion(f32[192,2304]{0,1:T(8,128)S(1)} %copy-done.3, s32[16384]{0:T(1024)S(1)} %copy-done.52, f32[16384,192]{1,0:T(8,128)} %bitcast.749), kind=kCustom, calls=%fused_computation.22 | custom fusion | flops 3145728 | bytes 37814272 | tf_op jit(solution)/shard_map/transpose(jvp(jit(_take)))/scatter-add | solution.py:44
  3984.5 90.2 %scatter_custom_fusion.9 = f32[192,2304]{0,1:T(8,128)} fusion(s32[16384]{0:T(1024)} %fusion.414, f32[16384,192]{1,0:T(8,128)} %bitcast.778, f32[]{:T(128)} %constant.124.clone.1), kind=kCustom, calls=%fused_computation.397 | custom fusion | flops 3145728 | bytes 1769984 | tf_op jit(solution)/shard_map/transpose(jvp(jit(_take)))/scatter-add | solution.py:44
  4074.8 89.0 %scatter_fusion.3 = f32[192,2304]{0,1:T(8,128)S(1)} fusion(f32[192,2304]{0,1:T(8,128)S(1)} %copy-done.4, s32[16384]{0:T(1024)S(1)} %copy-done.51, f32[16384,192]{1,0:T(8,128)} %bitcast.748), kind=kCustom, calls=%fused_computation.24 | custom fusion | flops 3145728 | bytes 37814272 | tf_op jit(solution)/shard_map/transpose(jvp(jit(_take)))/scatter-add | solution.py:44
  4167.1 89.7 %scatter_custom_fusion.11 = f32[192,2304]{0,1:T(8,128)} fusion(s32[16384]{0:T(1024)} %fusion.408, f32[16384,192]{1,0:T(8,128)} %bitcast.777, f32[]{:T(128)} %constant.124.clone.1), kind=kCustom, calls=%fused_computation.395 | custom fusion | flops 3145728 | bytes 1769984 | tf_op jit(solution)/shard_map/transpose(jvp(jit(_take)))/scatter-add | solution.py:44
  4256.8 91.1 %scatter_fusion.4 = f32[192,2304]{0,1:T(8,128)} fusion(f32[192,2304]{0,1:T(8,128)} %add_any.146, s32[16384]{0:T(1024)S(1)} %copy-done.50, f32[16384,192]{1,0:T(8,128)} %bitcast.747), kind=kCustom, calls=%fused_computation.26 | custom fusion | flops 3145728 | bytes 37814272 | tf_op jit(solution)/shard_map/transpose(jvp(jit(_take)))/scatter-add | solution.py:44
  4350.6 89.8 %scatter_custom_fusion.13 = f32[192,2304]{0,1:T(8,128)} fusion(s32[16384]{0:T(1024)} %fusion.402, f32[16384,192]{1,0:T(8,128)} %bitcast.776, f32[]{:T(128)} %constant.124.clone.1), kind=kCustom, calls=%fused_computation.393 | custom fusion | flops 3145728 | bytes 1769984 | tf_op jit(solution)/shard_map/transpose(jvp(jit(_take)))/scatter-add | solution.py:44
  4440.5 89.0 %scatter_fusion.5 = f32[192,2304]{0,1:T(8,128)S(1)} fusion(f32[192,2304]{0,1:T(8,128)S(1)} %add_any.147, s32[16384]{0:T(1024)S(1)} %copy-done.49, f32[16384,192]{1,0:T(8,128)} %bitcast.746), kind=kCustom, calls=%fused_computation.28 | custom fusion | flops 3145728 | bytes 37814272 | tf_op jit(solution)/shard_map/transpose(jvp(jit(_take)))/scatter-add | solution.py:44
  4532.9 91.3 %scatter_fusion.6 = f32[192,2304]{0,1:T(8,128)} fusion(f32[192,2304]{0,1:T(8,128)} %add_any.148, s32[16384]{0:T(1024)S(1)} %copy-done.48, f32[16384,192]{1,0:T(8,128)} %bitcast.745), kind=kCustom, calls=%fused_computation.30 | custom fusion | flops 3145728 | bytes 37814272 | tf_op jit(solution)/shard_map/transpose(jvp(jit(_take)))/scatter-add | solution.py:44
  4643.4 129.6 %all-reduce.42.cloned.1.call-done = (f32[768,3,192]{0,2,1:T(8,128)}, f32[192,2048]{0,1:T(8,128)}, f32[192,768]{1,0:T(8,128)}, f32[768,768]{1,0:T(8,128)}, f32[768,768]{1,0:T(8,128)}) async-done(((f32[768,3,192]{0,2,1:T(8,128)}, f32[192,2048]{0,1:T(8,128)}, f32[192,768]{1,0:T(8,128)}, f32[768,768]{1,0:T(8,128)}, f32[768,768]{1,0:T(8,128)}), (f32[768,3,192]{0,2,1:T(8,128)}, f32[192,2048]{0,1:T(8,128)}, ...) | async-done | bytes 8650768 | tf_op jit(solution)/shard_map/psum | solution.py:147
  4775.8 110.5 %reduce-scatter.11.cloned.1.call-done = f32[1,512,768]{2,1,0:T(8,128)} async-done(((f32[1,2048,768]{2,1,0:T(8,128)}), f32[1,512,768]{2,1,0:T(8,128)}) %reduce-scatter.11.cloned.1.call-update) | async-done | bytes 1572880 | tf_op jit(solution)/shard_map/reduce_scatter | solution.py:144
  (606 shorter events, 2197.2 us)
Async XLA Ops:
  7.2 1917.3 %copy-start = (bf16[768,768]{1,0:T(8,128)(2,1)S(1)}, bf16[768,768]{1,0:T(8,128)(2,1)}, u32[]{:S(2)}) copy-start(bf16[768,768]{1,0:T(8,128)(2,1)} %param.19) | copy-start | bytes 3538948
  7.2 1369.4 %all-gather.5.cloned.1.call-start = ((), (), s32[]{:S(2)}) async-start(), calls=%async_computation.4 | async-start | bytes 3932160 | tf_op jit(solution)/shard_map/all_gather | solution.py:75
  13.7 1842.7 %reduce-scatter.5.cloned.1.call-start = ((), (), s32[]{:S(2)}) async-start(), calls=%async_computation.5 | async-start | bytes 7864320 | tf_op jit(solution)/shard_map/reduce_scatter | solution.py:84
  1376.6 337.6 %copy-start.55 = (pred[128,128]{1,0:T(8,128)(4,1)}, pred[128,128]{1,0:T(8,128)(4,1)S(1)}, u32[]{:S(2)}) copy-start(pred[128,128]{1,0:T(8,128)(4,1)S(1)} %fusion.459) | copy-start | bytes 49156
  1383.5 90.5 %copy-start.22 = (f32[1,5,128,192]{2,1,3,0:T(8,128)}, f32[1,5,128,192]{2,1,3,0:T(8,128)S(1)}, u32[]{:S(2)}) copy-start(f32[1,5,128,192]{2,1,3,0:T(8,128)S(1)} %slice.143) | copy-start | bytes 1474564
  1386.3 154.4 %copy-start.18 = (f32[1,8,128,192]{2,1,3,0:T(8,128)}, f32[1,8,128,192]{2,1,3,0:T(8,128)S(1)}, u32[]{:S(2)}) copy-start(f32[1,8,128,192]{2,1,3,0:T(8,128)S(1)} %slice.140) | copy-start | bytes 2359300
  1742.7 113.6 %copy-start.9 = (bf16[1,512,768]{2,1,0:T(8,128)(2,1)S(1)}, bf16[1,512,768]{2,1,0:T(8,128)(2,1)}, u32[]{:S(2)}) copy-start(bf16[1,512,768]{2,1,0:T(8,128)(2,1)} %param.12) | copy-start | bytes 2359300
  1742.8 116.4 %copy-start.90 = (f32[768]{0:T(1024)S(1)}, f32[768]{0:T(1024)}, u32[]{:S(2)}) copy-start(f32[768]{0:T(1024)} %param.18) | copy-start | bytes 9220
  1742.8 181.7 %all-gather.7.cloned.1.call-start = ((), (), s32[]{:S(2)}) async-start(), calls=%async_computation.6 | async-start | bytes 3932160 | tf_op jit(solution)/shard_map/all_gather | solution.py:89
  1860.3 127.8 %all-gather.9.cloned.1.call-start = ((), (), s32[]{:S(2)}) async-start(), calls=%async_computation.8 | async-start | bytes 3932160 | tf_op jit(solution)/shard_map/all_gather | solution.py:90
  1860.9 251.4 %reduce-scatter.9.cloned.1.call-start = ((), (), s32[]{:S(2)}) async-start(), calls=%async_computation.9 | async-start | bytes 7864320 | tf_op jit(solution)/shard_map/reduce_scatter | solution.py:110
  2002.8 223.0 %reduce-scatter.7.cloned.1.call-start = ((), (), s32[]{:S(2)}) async-start(), calls=%async_computation.7 | async-start | bytes 7864320 | tf_op jit(solution)/shard_map/reduce_scatter | solution.py:100
  2013.4 282.8 %all-gather.11.cloned.1.call-start = ((), (), s32[]{:S(2)}) async-start(), calls=%async_computation.10 | async-start | bytes 3932160 | tf_op jit(solution)/shard_map/all_gather | solution.py:123
  2115.4 115.4 %copy-start.24 = (bf16[1,512,768]{2,1,0:T(8,128)(2,1)S(1)}, bf16[1,512,768]{2,1,0:T(8,128)(2,1)}, u32[]{:S(2)}) copy-start(bf16[1,512,768]{2,1,0:T(8,128)(2,1)} %param.21) | copy-start | bytes 2359300
  2232.0 2541.1 %all-reduce.42.cloned.1.call-start = ((), (), s32[]{:S(2)}) async-start(), calls=%async_computation.12 | async-start | bytes 18350080 | tf_op jit(solution)/shard_map/psum | solution.py:147
  3616.4 93.5 %copy-start.53 = (s32[16384]{0:T(1024)S(1)}, s32[16384]{0:T(1024)}, u32[]{:S(2)}) copy-start(s32[16384]{0:T(1024)} %fusion.429) | copy-start | bytes 196612
  3619.9 90.1 %copy-start.2 = (f32[192,2304]{0,1:T(8,128)S(1)}, f32[192,2304]{0,1:T(8,128)}, u32[]{:S(2)}) copy-start(f32[192,2304]{0,1:T(8,128)} %add_any.143) | copy-start | bytes 5308420
  3798.9 93.2 %copy-start.52 = (s32[16384]{0:T(1024)S(1)}, s32[16384]{0:T(1024)}, u32[]{:S(2)}) copy-start(s32[16384]{0:T(1024)} %fusion.423) | copy-start | bytes 196612
  3981.1 93.7 %copy-start.51 = (s32[16384]{0:T(1024)S(1)}, s32[16384]{0:T(1024)}, u32[]{:S(2)}) copy-start(s32[16384]{0:T(1024)} %fusion.417) | copy-start | bytes 196612
  3984.5 90.2 %copy-start.4 = (f32[192,2304]{0,1:T(8,128)S(1)}, f32[192,2304]{0,1:T(8,128)}, u32[]{:S(2)}) copy-start(f32[192,2304]{0,1:T(8,128)} %add_any.145) | copy-start | bytes 5308420
  4350.6 89.8 %copy-start.49 = (s32[16384]{0:T(1024)S(1)}, s32[16384]{0:T(1024)}, u32[]{:S(2)}) copy-start(s32[16384]{0:T(1024)} %fusion.405) | copy-start | bytes 196612
  4532.9 91.3 %copy-start.17 = (f32[192,2304]{0,1:T(8,128)S(1)}, f32[192,2304]{0,1:T(8,128)}, u32[]{:S(2)}) copy-start(f32[192,2304]{0,1:T(8,128)} %scatter_custom_fusion.15) | copy-start | bytes 5308420
  4532.9 91.3 %copy-start.99 = (s32[192]{0:T(256)S(1)}, s32[192]{0:T(256)}, u32[]{:S(2)}) copy-start(s32[192]{0:T(256)} %copy-done.98) | copy-start | bytes 2308
  4637.6 248.7 %reduce-scatter.11.cloned.1.call-start = ((), (), s32[]{:S(2)}) async-start(), calls=%async_computation.11 | async-start | bytes 7864320 | tf_op jit(solution)/shard_map/reduce_scatter | solution.py:144
  4643.4 242.9 %copy-start.10 = (bf16[1,512,768]{2,1,0:T(8,128)(2,1)S(1)}, bf16[1,512,768]{2,1,0:T(8,128)(2,1)}, u32[]{:S(2)}) copy-start(bf16[1,512,768]{2,1,0:T(8,128)(2,1)} %param.12) | copy-start | bytes 2359300
  4643.4 242.9 %copy-start.88 = (f32[512]{0:T(512)S(1)}, f32[512]{0:T(512)}, u32[]{:S(2)}) copy-start(f32[512]{0:T(512)} %copy-done.87) | copy-start | bytes 6148
  4643.4 242.9 %copy-start.89 = (f32[768]{0:T(1024)S(1)}, f32[768]{0:T(1024)}, u32[]{:S(2)}) copy-start(f32[768]{0:T(1024)} %param.13) | copy-start | bytes 9220
  4773.0 115.3 %copy-start.96 = (f32[512]{0:T(512)S(1)}, f32[512]{0:T(512)}, u32[]{:S(2)}) copy-start(f32[512]{0:T(512)} %copy-done.95) | copy-start | bytes 6148
  4773.0 115.3 %copy-start.92 = (f32[512]{0:T(512)S(1)}, f32[512]{0:T(512)}, u32[]{:S(2)}) copy-start(f32[512]{0:T(512)} %copy-done.91) | copy-start | bytes 6148
  4775.8 113.3 %copy-start.97 = (f32[768]{0:T(1024)S(1)}, f32[768]{0:T(1024)}, u32[]{:S(2)}) copy-start(f32[768]{0:T(1024)} %get-tuple-element.82) | copy-start | bytes 9220
  4775.8 154.2 %copy-start.25 = (bf16[1,512,768]{2,1,0:T(8,128)(2,1)S(1)}, bf16[1,512,768]{2,1,0:T(8,128)(2,1)}, u32[]{:S(2)}) copy-start(bf16[1,512,768]{2,1,0:T(8,128)(2,1)} %param.21) | copy-start | bytes 2359300
  4775.8 154.2 %copy-start.94 = (f32[512]{0:T(512)S(1)}, f32[512]{0:T(512)}, u32[]{:S(2)}) copy-start(f32[512]{0:T(512)} %copy-done.93) | copy-start | bytes 6148
  (151 other events, 3378.9 us)
Sparse Core Ops, SparseCore 0:
  13.8 66.1 all-gather.4
  1742.9 113.4 reduce-scatter.4
  1860.5 64.0 all-gather.6
  1925.9 62.1 all-gather.8
  2002.9 109.3 reduce-scatter.8
  2114.5 111.2 reduce-scatter.6
  2232.1 64.0 all-gather.10
  4637.8 135.1 all-reduce.41
  4775.4 110.8 reduce-scatter.10
where the time goes:
time: 4990 us; the launch traced here: 4950 us
  local copies, waits for them, and re-layouts  1670 us (33%)
  other arithmetic  1520 us (30%)
  matrix products  983 us (20%)
  waiting for transfers between devices  720 us (14%)
    scatter-add x16, other arithmetic, causal_conv(): toeplitz = jnp.take(padded, offset + lag_index * block_width, axis=1)  1440 us
    gather x32, local copies, waits for them, and re-layouts, causal_conv(): toeplitz = jnp.take(padded, offset + lag_index * block_width, axis=1)  1340 us
    dot_general x48, matrix products, causal_conv(): jnp.einsum('snbc,crb->snrc', shifted, toeplitz, precision=lax.Precision.H...  914 us
    dot_general x16, local copies, waits for them, and re-layouts, causal_conv(): jnp.einsum('snbc,crb->snrc', shifted, toeplitz, precision=lax.Precision.H...  282 us
    psum x1, waiting for transfers between devices, body(): lax.psum((w_in_grad, kernel_grad, w_out_grad, up_projection_gradient, dow...  130 us
    reduce_scatter x1, waiting for transfers between devices, body(): lax.psum_scatter(partial_output_rows, 'mp', scatter_dimension=1, tiled=True)  114 us
    reduce_scatter x1, waiting for transfers between devices, body(): lax.psum_scatter(first_terms, 'mp', scatter_dimension=1, tiled=True)  111 us
    reduce_scatter x1, waiting for transfers between devices, body(): lax.psum_scatter(down_projection_terms, 'mp', scatter_dimension=1, tiled=...  110 us
  transfers between devices with their start and end apart: 9, of which 8 were waited for; matrix products, arithmetic and copies ran while one was open for 29% of the time, Pallas kernels for 0%

commit v1 on v0

v1 whole, which is shorter than its diff:
```python
import math
from functools import partial

import jax
import jax.numpy as jnp
import numpy as np
from jax import lax
from jax.experimental import pallas as pl
from jax.experimental.pallas import tpu as pltpu
from jax.sharding import PartitionSpec as P

LANES = 128
ROWS = 16
BASE = 256
f32 = jnp.float32
bf16 = jnp.bfloat16


def dft_tables(length):
    radix = length // BASE
    spot = np.arange(BASE)
    angle = 2 * np.pi * (np.outer(spot, spot) % BASE) / BASE
    cos, sin = np.cos(angle), np.sin(angle)
    matrix = np.block([[cos, -sin], [sin, cos]]).astype(np.float32)
    high = matrix.astype(jnp.bfloat16)
    low = (matrix - high.astype(np.float32)).astype(jnp.bfloat16)
    turn = 2 * np.pi * np.outer(np.arange(radix) + 0.25, spot) / length
    twiddle = np.stack([np.cos(turn), np.sin(turn)]).astype(np.float32)
    return high, low, twiddle


def times(re, im, angle):
    c, s = math.cos(angle), math.sin(angle)
    if abs(s) < 1e-12:
        return (re, im) if c > 0 else (-re, -im)
    if abs(c) < 1e-12:
        return (-im, re) if s > 0 else (im, -re)
    if abs(abs(c) - abs(s)) < 1e-12:
        a = abs(c)
        sc, ss = (a if c > 0 else -a), (1.0 if (s > 0) == (c > 0) else -1.0)
        if ss > 0:
            return (re - im) * sc, (re + im) * sc
        return (re + im) * sc, (im - re) * sc
    return re * c - im * s, re * s + im * c


def radix_dft(re, im, sign):
    n = len(re)
    if n == 1:
        return re, im
    er, ei = radix_dft(re[0::2], im[0::2], sign)
    odr, odi = radix_dft(re[1::2], im[1::2], sign)
    lo_r, lo_i, hi_r, hi_i = [], [], [], []
    for k in range(n // 2):
        tr, ti = times(odr[k], odi[k], sign * 2 * math.pi * k / n)
        lo_r.append(er[k] + tr)
        lo_i.append(ei[k] + ti)
        hi_r.append(er[k] - tr)
        hi_i.append(ei[k] - ti)
    return lo_r + hi_r, lo_i + hi_i


def split_in(load, twiddle_ref, store, radix, channels):
    def step(tile, carry):
        rows = pl.ds(pl.multiple_of(tile * ROWS, ROWS), ROWS)
        for half in range(BASE // LANES):
            lanes = slice(half * LANES, (half + 1) * LANES)
            re, im = [], []
            for block in range(radix):
                x = load(rows, block, half)
                angle = -2 * math.pi * block * 0.25 / radix
                re.append(x * math.cos(angle))
                im.append(x * math.sin(angle))
            re, im = radix_dft(re, im, -1)
            for k in range(radix):
                c = twiddle_ref[0, k : k + 1, lanes]
                s = twiddle_ref[1, k : k + 1, lanes]
                store(rows, k, half, re[k] * c + im[k] * s, im[k] * c - re[k] * s)
        return carry

    lax.fori_loop(0, channels // ROWS, step, 0)


def split_out(load, twiddle_ref, store, radix, channels, length):
    def step(tile, carry):
        rows = pl.ds(pl.multiple_of(tile * ROWS, ROWS), ROWS)
        for half in range(BASE // LANES):
            lanes = slice(half * LANES, (half + 1) * LANES)
            re, im = [], []
            for k in range(radix):
                vr, vi = load(rows, k, half)
                c = twiddle_ref[0, k : k + 1, lanes]
                s = twiddle_ref[1, k : k + 1, lanes]
                re.append(vr * c - vi * s)
                im.append(vr * s + vi * c)
            re, im = radix_dft(re, im, 1)
            for block in range(radix):
                angle = 2 * math.pi * block * 0.25 / radix
                store(
                    rows,
                    block,
                    half,
                    re[block] * (math.cos(angle) / length) - im[block] * (math.sin(angle) / length),
                )
        return carry

    lax.fori_loop(0, channels // ROWS, step, 0)


def forward_dot(z, matrix):
    return jnp.dot(z, matrix, preferred_element_type=f32)


def inverse_dot(y, matrix):
    return lax.dot_general(y, matrix, (((1,), (1,)), ((), ())), preferred_element_type=f32)


def product_loop(a_load, b_load, store, total_rows, conj):
    def step(tile, carry):
        rows = pl.ds(pl.multiple_of(tile * ROWS, ROWS), ROWS)
        for half in range(BASE // LANES):
            cr = slice(half * LANES, (half + 1) * LANES)
            ci = slice(BASE + half * LANES, BASE + (half + 1) * LANES)
            ar, ai = a_load(rows, cr), a_load(rows, ci)
            br, bi = b_load(rows, cr), b_load(rows, ci)
            if conj:
                store(rows, cr, ar * br + ai * bi)
                store(rows, ci, ai * br - ar * bi)
            else:
                store(rows, cr, ar * br - ai * bi)
                store(rows, ci, ai * br + ar * bi)
        return carry

    lax.fori_loop(0, total_rows // ROWS, step, 0)


def cut(ref, rows, block, half):
    width = ref.shape[-1]
    start = block * BASE + half * LANES
    return ref[start // width, rows, start % width : start % width + LANES]


def put(ref, rows, block, half, value):
    width = ref.shape[-1]
    start = block * BASE + half * LANES
    ref[start // width, rows, start % width : start % width + LANES] = value.astype(ref.dtype)


def rowshift(rows, k, channels):
    return pl.ds(pl.multiple_of(rows.start + k * channels, ROWS), ROWS)


def into_scratch(ref, channels):
    def store(rows, k, half, re, im):
        at = rowshift(rows, k, channels)
        ref[at, half * LANES : (half + 1) * LANES] = re.astype(ref.dtype)
        ref[at, BASE + half * LANES : BASE + (half + 1) * LANES] = im.astype(ref.dtype)

    return store


def from_scratch(ref, channels):
    def load(rows, k, half):
        at = rowshift(rows, k, channels)
        return (
            ref[at, half * LANES : (half + 1) * LANES].astype(f32),
            ref[at, BASE + half * LANES : BASE + (half + 1) * LANES].astype(f32),
        )

    return load


def filter_kernel(f_ref, high_ref, low_ref, twiddle_ref, spec_ref, zh, zl, *, radix, channels):
    def store(rows, k, half, re, im):
        at = rowshift(rows, k, channels)
        for value, base in ((re, 0), (im, BASE)):
            lanes = slice(base + half * LANES, base + (half + 1) * LANES)
            top = value.astype(bf16)
            zh[at, lanes] = top
            zl[at, lanes] = (value - top.astype(f32)).astype(bf16)

    split_in(partial(cut, f_ref), twiddle_ref, store, radix, channels)
    spec_ref[...] = (
        forward_dot(zh[...], high_ref[...])
        + forward_dot(zl[...], high_ref[...])
        + forward_dot(zh[...], low_ref[...])
    )


def tile_load(ref):
    return lambda rows, lanes: ref[rows, lanes].astype(f32)


def tile_store(ref):
    def store(rows, lanes, value):
        ref[rows, lanes] = value.astype(ref.dtype)

    return store


def conv_kernel(
    u_ref, fspec_ref, high_ref, twiddle_ref, out_ref, uspec_ref, z, y, big, *, radix, channels, length
):
    load = lambda rows, block, half: cut(u_ref, rows, block, half).astype(f32)
    split_in(load, twiddle_ref, into_scratch(z, channels), radix, channels)
    big[...] = forward_dot(z[...], high_ref[...])
    uspec_ref[...] = big[...].astype(uspec_ref.dtype)
    product_loop(tile_load(big), tile_load(fspec_ref), tile_store(y), radix * channels, False)
    big[...] = inverse_dot(y[...], high_ref[...])
    split_out(from_scratch(big, channels), twiddle_ref, partial(put, out_ref), radix, channels, length)


def conv_back_kernel(
    g_ref, fspec_ref, uspec_ref, high_ref, twiddle_ref, mixed_ref, filt_ref, z, y, big, spec, *, radix, channels, length
):
    load = lambda rows, block, half: cut(g_ref, rows, block, half).astype(f32)
    split_in(load, twiddle_ref, into_scratch(z, channels), radix, channels)
    spec[...] = forward_dot(z[...], high_ref[...])
    product_loop(tile_load(spec), tile_load(fspec_ref), tile_store(y), radix * channels, True)
    big[...] = inverse_dot(y[...], high_ref[...])
    split_out(from_scratch(big, channels), twiddle_ref, partial(put, mixed_ref), radix, channels, length)
    product_loop(tile_load(spec), tile_load(uspec_ref), tile_store(y), radix * channels, True)
    big[...] = inverse_dot(y[...], high_ref[...])
    split_out(from_scratch(big, channels), twiddle_ref, partial(put, filt_ref), radix, channels, length)


VM = pl.BlockSpec(memory_space=pltpu.VMEM)


def filter_spectrum(filt, tables):
    high, low, twiddle = tables
    channels, length = filt.shape[1], filt.shape[0] * filt.shape[2]
    radix = length // BASE
    rows = radix * channels
    return pl.pallas_call(
        partial(filter_kernel, radix=radix, channels=channels),
        out_shape=jax.ShapeDtypeStruct((rows, 2 * BASE), f32),
        in_specs=[VM] * 4,
        out_specs=VM,
        scratch_shapes=[pltpu.VMEM((rows, 2 * BASE), bf16)] * 2,
        name="filter_spectrum",
    )(filt, high, low, twiddle)


def conv_forward(u, fspec, tables, out_dtype):
    high, _, twiddle = tables
    parts, channels, width = u.shape
    length = parts * width
    radix = length // BASE
    rows = radix * channels
    return pl.pallas_call(
        partial(conv_kernel, radix=radix, channels=channels, length=length),
        out_shape=(
            jax.ShapeDtypeStruct((parts, channels, width), out_dtype),
            jax.ShapeDtypeStruct((rows, 2 * BASE), bf16),
        ),
        in_specs=[VM] * 4,
        out_specs=(VM, VM),
        scratch_shapes=[pltpu.VMEM((rows, 2 * BASE), bf16)] * 2 + [pltpu.VMEM((rows, 2 * BASE), f32)],
        name="conv_forward",
    )(u, fspec, high, twiddle)


def conv_backward(g, fspec, uspec, tables, out_dtype, filt_dtype):
    high, _, twiddle = tables
    parts, channels, width = g.shape
    length = parts * width
    radix = length // BASE
    rows = radix * channels
    return pl.pallas_call(
        partial(conv_back_kernel, radix=radix, channels=channels, length=length),
        out_shape=(
            jax.ShapeDtypeStruct((parts, channels, width), out_dtype),
            jax.ShapeDtypeStruct((1, channels, length), filt_dtype),
        ),
        in_specs=[VM] * 5,
        out_specs=(VM, VM),
        scratch_shapes=[pltpu.VMEM((rows, 2 * BASE), bf16)] * 2 + [pltpu.VMEM((rows, 2 * BASE), f32)] * 2,
        name="conv_backward",
    )(g, fspec, uspec, high, twiddle)


thresh = 0.003
epsilon = 1e-05


def layer_norm(values, scale_vec):
    centered = values - jnp.mean(values, axis=-1, keepdims=True)
    spread = jnp.mean(centered * centered, axis=-1, keepdims=True)
    return centered * lax.rsqrt(spread + epsilon) * scale_vec


def gelu_tanh(values):
    return jax.nn.gelu(values, approximate=True)


def shrink_pool(kernel, pad_len):
    shrunk = jax.nn.relu(kernel - thresh) - jax.nn.relu(-kernel - thresh)
    padded = jnp.pad(shrunk, ((0, 0), (1, 1)))
    pooled = (padded[:, :-2] + padded[:, 1:-1] + padded[:, 2:]) / 3.0
    positions = lax.broadcasted_iota(jnp.int32, pooled.shape, 1)
    return jnp.where(positions < (pooled.shape[1] - pad_len)[:, None], pooled, 0.0)


def body(
    tables,
    tokens,
    gain_first,
    input_weight,
    kernel,
    pad_len,
    output_weight,
    gain_second,
    up_weight,
    down_weight,
    cotangent,
):
    start_rows = tokens.astype(f32)
    filt, filter_back = jax.vjp(partial(shrink_pool, pad_len=pad_len), kernel)
    seqs = tokens.shape[0]
    length = tokens.shape[1] * lax.axis_size("mp")
    fspec = filter_spectrum(jnp.pad(filt, ((0, 0), (0, length - filt.shape[1])))[None], tables)
    normed_one, first_back = jax.vjp(layer_norm, start_rows, gain_first)
    normed_low = normed_one.astype(bf16)
    whole = lax.all_gather(normed_low, "mp", axis=1, tiled=True)
    proj = jnp.einsum("spd,dkc->skcp", whole, input_weight, preferred_element_type=f32)
    value, gate_one, gate_two = proj[:, 0], proj[:, 1], proj[:, 2]
    mixed_in = (value * gate_one).astype(bf16)
    conv_runs = [conv_forward(mixed_in[s][None], fspec, tables, f32) for s in range(seqs)]
    conv = jnp.stack([run[0][0] for run in conv_runs])
    mixer_low = (gate_two * conv).astype(bf16)
    partial_rows = jnp.einsum("scp,cd->spd", mixer_low, output_weight, preferred_element_type=f32)
    mixer_sum = lax.psum_scatter(partial_rows.astype(bf16), "mp", scatter_dimension=1, tiled=True)
    residual_one = start_rows + mixer_sum.astype(f32)
    normed_two, second_back = jax.vjp(layer_norm, residual_one, gain_second)
    second_low = normed_two.astype(bf16)
    second_whole = lax.all_gather(second_low, "mp", axis=1, tiled=True)
    grad_whole = lax.all_gather(cotangent, "mp", axis=1, tiled=True)
    hidden_pre = jnp.einsum("spd,df->spf", second_whole, up_weight, preferred_element_type=f32)
    hidden_act, act_back = jax.vjp(gelu_tanh, hidden_pre)
    act_low = hidden_act.astype(bf16)
    down_terms = jnp.einsum("spf,fd->spd", act_low, down_weight, preferred_element_type=f32)
    block_out = residual_one + lax.psum_scatter(
        down_terms.astype(bf16), "mp", scatter_dimension=1, tiled=True
    ).astype(f32)
    grad_act = jnp.einsum("spd,fd->spf", grad_whole, down_weight, preferred_element_type=f32)
    grad_pre = act_back(grad_act)[0].astype(bf16)
    norm_terms = jnp.einsum("spf,df->spd", grad_pre, up_weight, preferred_element_type=f32)
    grad_norm_two = lax.psum_scatter(
        norm_terms.astype(bf16), "mp", scatter_dimension=1, tiled=True
    ).astype(f32)
    up_grad = jnp.einsum("spd,spf->df", second_whole, grad_pre, preferred_element_type=f32)
    down_grad = jnp.einsum("spf,spd->fd", act_low, grad_whole, preferred_element_type=f32)
    grad_mid_norm, gain_second_grad = second_back(grad_norm_two)
    grad_mid = cotangent.astype(f32) + grad_mid_norm
    mid_whole = lax.all_gather(grad_mid.astype(bf16), "mp", axis=1, tiled=True)
    w_out_grad = jnp.einsum("scp,spd->cd", mixer_low, mid_whole, preferred_element_type=f32)
    grad_mixer = jnp.einsum("spd,cd->scp", mid_whole, output_weight, preferred_element_type=f32)
    grad_conv = (grad_mixer * gate_two).astype(bf16)
    back_runs = [
        conv_backward(grad_conv[s][None], fspec, conv_runs[s][1], tables, f32, f32) for s in range(seqs)
    ]
    grad_mixed = jnp.stack([run[0][0] for run in back_runs])
    filt_grad = sum(run[1][0] for run in back_runs)[:, : kernel.shape[1]]
    (kernel_grad,) = filter_back(filt_grad)
    proj_grad = jnp.stack(
        [grad_mixed * gate_one, grad_mixed * value, grad_mixer * conv], axis=1
    ).astype(bf16)
    w_in_grad = jnp.einsum("spd,skcp->dkc", whole, proj_grad, preferred_element_type=f32)
    first_terms = jnp.einsum("skcp,dkc->spd", proj_grad, input_weight, preferred_element_type=f32)
    grad_norm_one = lax.psum_scatter(
        first_terms.astype(bf16), "mp", scatter_dimension=1, tiled=True
    ).astype(f32)
    grad_start, gain_first_grad = first_back(grad_norm_one)
    grad_tokens = grad_mid + grad_start
    weight_sums = lax.psum((w_in_grad, kernel_grad, w_out_grad, up_grad, down_grad), "dp")
    gain_sums = lax.psum((gain_first_grad, gain_second_grad), ("dp", "mp"))
    return (
        block_out.astype(bf16),
        grad_tokens,
        gain_sums[0],
        weight_sums[0],
        weight_sums[1],
        weight_sums[2],
        gain_sums[1],
        weight_sums[3],
        weight_sums[4],
    )


def solution(mesh):
    in_specs = (
        P("dp", "mp", None),
        P(),
        P(None, None, "mp"),
        P("mp", None),
        P("mp"),
        P("mp", None),
        P(),
        P(None, "mp"),
        P("mp", None),
        P("dp", "mp", None),
    )
    out_specs = (
        P("dp", "mp", None),
        P("dp", "mp", None),
        P(),
        P(None, None, "mp"),
        P("mp", None),
        P("mp", None),
        P(),
        P(None, "mp"),
        P("mp", None),
    )

    def program(tokens, *rest):
        tables = tuple(jnp.asarray(t) for t in dft_tables(tokens.shape[1]))
        inner = jax.shard_map(
            body, mesh=mesh, in_specs=((P(), P(), P()),) + in_specs, out_specs=out_specs, check_vma=False
        )
        return inner(tables, tokens, *rest)

    return program
```

time: 4990 us -> 741 us (0.15)
  local copies, waits for them, and re-layouts: 1670 us -> 19.9 us
  other arithmetic: 1520 us -> 33.7 us
  matrix products: 983 us -> 61 us
  waiting for transfers between devices: 720 us -> 533 us
    scatter-add x16 -> x0, other arithmetic: 1440 us -> none  [causal_conv(): toeplitz = jnp.take(padded, offset + lag_index * block_width, axis=1)]
    gather x32 -> x0, local copies, waits for them, and re-layouts: 1340 us -> none  [causal_conv(): toeplitz = jnp.take(padded, offset + lag_index * block_width, axis=1)]
    dot_general x58 -> x11, matrix products: 975 us -> 57.1 us  [the longest x1 8.32 us: body(): jnp.einsum('spd,fd->spf', grad_whole, down_weight, preferred_element_type...]
    dot_general x16 -> x0, local copies, waits for them, and re-layouts: 282 us -> none  [causal_conv(): jnp.einsum('snbc,crb->snrc', shifted, toeplitz, precision=lax.Precision.H...]
    reduce_scatter x4, waiting for transfers between devices: 432 us -> 204 us  [the longest x1 60.4 us: body(): lax.psum_scatter(down_terms.astype(bf16), 'mp', scatter_dimension=1, tile...]
    all_gather x4, waiting for transfers between devices: 157 us -> 239 us  [the longest x1 63.6 us: body(): mid_whole = lax.all_gather(grad_mid.astype(bf16), 'mp', axis=1, tiled=True)]
  transfers between devices with their start and end apart: 9 -> 9, of which waited for: 8 -> 9; matrix products, arithmetic and copies ran while one was open for 29% -> 7% of each run, Pallas kernels for 0% -> 1%
where the time goes in v1:
time: 741 us; the launch traced here: 733 us
  waiting for transfers between devices  533 us (72%)
  matrix products  61 us (8%)
  blocking collectives  41.5 us (6%)
  other arithmetic  33.7 us (5%)
  Pallas kernels  28.4 us (4%)
  local copies, waits for them, and re-layouts  19.9 us (3%)
  between operations  14.7 us (2%)
    psum x1, waiting for transfers between devices, body(): lax.psum((w_in_grad, kernel_grad, w_out_grad, up_grad, down_grad), 'dp')  89.1 us
    all_gather x1, waiting for transfers between devices, body(): mid_whole = lax.all_gather(grad_mid.astype(bf16), 'mp', axis=1, tiled=True)  63.6 us
    all_gather x1, waiting for transfers between devices, body(): second_whole = lax.all_gather(second_low, 'mp', axis=1, tiled=True)  62.9 us
    reduce_scatter x1, waiting for transfers between devices, body(): lax.psum_scatter(down_terms.astype(bf16), 'mp', scatter_dimension=1, tile...  60.4 us
    reduce_scatter x1, waiting for transfers between devices, body(): lax.psum_scatter(partial_rows.astype(bf16), 'mp', scatter_dimension=1, ti...  59 us
    all_gather x1, waiting for transfers between devices, body(): grad_whole = lax.all_gather(cotangent, 'mp', axis=1, tiled=True)  56.5 us
    all_gather x1, waiting for transfers between devices, body(): whole = lax.all_gather(normed_low, 'mp', axis=1, tiled=True)  56.2 us
    reduce_scatter x1, waiting for transfers between devices, body(): lax.psum_scatter(norm_terms.astype(bf16), 'mp', scatter_dimension=1, tile...  49.2 us
  transfers between devices with their start and end apart: 9, of which 9 were waited for; matrix products, arithmetic and copies ran while one was open for 7% of the time, Pallas kernels for 1%

profile of v1, /device:TPU:0, one launch (start us, length us, event | category | flops | bytes accessed | tf_op | source)
XLA Modules:
  0.0 732.7 jit_solution(5985651600899287621)
XLA Ops:
  15.5 7.4 %filter_spectrum.1.fspec_ref = f32[1536,512]{1,0:T(8,128)} custom-call(f32[1,192,2048]{2,1,0:T(8,128)} %fusion.41.f_ref, bf16[512,512]{1,0:T(8,128)(2,1)} %constant.54.clone.high_ref, bf16[512,512]{1,0:T(8,128)(2,1)} %constant.55.clone.low_ref, f32[2,8,256]{2,1,0:T(8,128)} %constant.56.clone.twiddle_ref), custom_call_target="tpu_custom_call" | custom-call | tf_op jit(solution)/shard_map/filter_spectrum/pallas_call | solution.py:235
  22.9 56.2 %all-gather.5.cloned.1.call-done = bf16[1,2048,768]{2,1,0:T(8,128)(2,1)} async-done(((bf16[1,512,768]{2,1,0:T(8,128)(2,1)}), bf16[1,2048,768]{2,1,0:T(8,128)(2,1)}) %all-gather.5.cloned.1.call-update) | async-done | bytes 3145744 | tf_op jit(solution)/shard_map/all_gather | solution.py:325
  79.1 3.9 fusion.21
  83.0 2.2 copy-done.5
  86.3 8.7 %conv_forward.1 = (f32[1,192,2048]{2,1,0:T(8,128)}, bf16[1536,512]{1,0:T(8,128)(2,1)}) custom-call(bf16[1,192,2048]{2,1,0:T(8,128)(2,1)} %multiply_convert_fusion.4.u_ref, f32[1536,512]{1,0:T(8,128)} %filter_spectrum.1.fspec_ref, bf16[512,512]{1,0:T(8,128)(2,1)} %constant.54.clone.high_ref, f32[2,8,256]{2,1,0:T(8,128)} %constant.56.clone.twiddle_ref), custom_call_target="tpu_custom_call" | custom-call | tf_op jit(solution)/shard_map/conv_forward/pallas_call | solution.py:251
  95.1 2.1 fusion.56
  98.1 2.7 fusion.23
  100.8 59.0 %reduce-scatter.5.cloned.1.call-done = bf16[1,512,768]{2,1,0:T(8,128)(2,1)} async-done(((bf16[1,2048,768]{2,1,0:T(8,128)(2,1)}), bf16[1,512,768]{2,1,0:T(8,128)(2,1)}) %reduce-scatter.5.cloned.1.call-update) | async-done | bytes 786448 | tf_op jit(solution)/shard_map/reduce_scatter | solution.py:333
  163.9 62.9 %all-gather.7.cloned.1.call-done = bf16[1,2048,768]{2,1,0:T(8,128)(2,1)} async-done(((bf16[1,512,768]{2,1,0:T(8,128)(2,1)}), bf16[1,2048,768]{2,1,0:T(8,128)(2,1)}) %all-gather.7.cloned.1.call-update) | async-done | bytes 3145744 | tf_op jit(solution)/shard_map/all_gather | solution.py:337
  226.7 7.1 fusion.19
  233.9 56.5 %all-gather.9.cloned.1.call-done = bf16[1,2048,768]{2,1,0:T(8,128)(2,1)} async-done(((bf16[1,512,768]{2,1,0:T(8,128)(2,1)}), bf16[1,2048,768]{2,1,0:T(8,128)(2,1)}) %all-gather.9.cloned.1.call-update) | async-done | bytes 3145744 | tf_op jit(solution)/shard_map/all_gather | solution.py:338
  290.3 8.3 %fusion.6 = bf16[2048,768]{1,0:T(8,128)(2,1)S(1)} fusion(f32[2048,768]{1,0:T(8,128)} %fusion.19, bf16[768,768]{1,0:T(8,128)(2,1)} %param.21, bf16[1,2048,768]{2,1,0:T(8,128)(2,1)} %all-gather.9.cloned.1.call-done), kind=kOutput, calls=%fused_computation.8 | convolution fusion | flops 2447376384 | bytes 13762560 | tf_op jit(solution)/shard_map/spd,fd->spf/dot_general | solution.py:346
  300.4 4.1 fusion.25
  305.7 8.3 %fusion.24 = bf16[1,2048,768]{2,1,0:T(8,128)(2,1)} fusion(bf16[768,768]{1,0:T(8,128)(2,1)S(1)} %copy-done.40, f32[2048,768]{1,0:T(8,128)} %fusion.19), kind=kOutput, calls=%fused_computation.31 | convolution fusion | flops 2431647744 | bytes 10616832 | tf_op jit(solution)/shard_map/spf,fd->spd/dot_general | solution.py:342
  314.3 49.2 %reduce-scatter.9.cloned.1.call-done = bf16[1,512,768]{2,1,0:T(8,128)(2,1)} async-done(((bf16[1,2048,768]{2,1,0:T(8,128)(2,1)}), bf16[1,512,768]{2,1,0:T(8,128)(2,1)}) %reduce-scatter.9.cloned.1.call-update) | async-done | bytes 786448 | tf_op jit(solution)/shard_map/reduce_scatter | solution.py:349
  365.7 60.4 %reduce-scatter.7.cloned.1.call-done = bf16[1,512,768]{2,1,0:T(8,128)(2,1)} async-done(((bf16[1,2048,768]{2,1,0:T(8,128)(2,1)}), bf16[1,512,768]{2,1,0:T(8,128)(2,1)}) %reduce-scatter.7.cloned.1.call-update) | async-done | bytes 786448 | tf_op jit(solution)/shard_map/reduce_scatter | solution.py:343
  426.0 2.8 fusion.62
  431.2 63.6 %all-gather.11.cloned.1.call-done = bf16[1,2048,768]{2,1,0:T(8,128)(2,1)} async-done(((bf16[1,512,768]{2,1,0:T(8,128)(2,1)}), bf16[1,2048,768]{2,1,0:T(8,128)(2,1)}) %all-gather.11.cloned.1.call-update) | async-done | bytes 3145744 | tf_op jit(solution)/shard_map/all_gather | solution.py:356
  494.9 3.1 fusion.48
  497.9 2.8 fusion.57.g_ref
  500.7 12.2 %conv_backward.1 = (f32[1,192,2048]{2,1,0:T(8,128)}, f32[1,192,2048]{2,1,0:T(8,128)}) custom-call(bf16[1,192,2048]{2,1,0:T(8,128)(2,1)} %fusion.57.g_ref, f32[1536,512]{1,0:T(8,128)} %filter_spectrum.1.fspec_ref, bf16[1536,512]{1,0:T(8,128)(2,1)} %get-tuple-element.14.uspec_ref, bf16[512,512]{1,0:T(8,128)(2,1)} %constant.54.clone.high_ref, ...), custom_call_target="tpu_custom_call" | custom-call | tf_op jit(solution)/shard_map/conv_backward/pallas_call | solution.py:270
  512.9 2.9 multiply_convert_fusion.2
  515.9 4.1 fusion.26
  520.2 7.1 fusion.17
  527.3 7.6 %fusion.13 = f32[768,768]{1,0:T(8,128)} fusion(bf16[1,2048,768]{2,1,0:T(8,128)(2,1)S(1)} %copy-done.39, f32[2048,768]{1,0:T(8,128)} %fusion.19), kind=kOutput, calls=%fused_computation.20 | convolution fusion | flops 2430074880 | bytes 11796480 | tf_op jit(solution)/shard_map/spf,spd->fd/dot_general | solution.py:353
  540.7 3.2 fusion.7
  544.0 35.0 %reduce-scatter.11.cloned.1.call-done = bf16[1,512,768]{2,1,0:T(8,128)(2,1)} async-done(((bf16[1,2048,768]{2,1,0:T(8,128)(2,1)}), bf16[1,512,768]{2,1,0:T(8,128)(2,1)}) %reduce-scatter.11.cloned.1.call-update) | async-done | bytes 786448 | tf_op jit(solution)/shard_map/reduce_scatter | solution.py:371
  580.7 2.1 fusion.45
  582.8 41.5 %all-reduce.4 = (f32[768]{0:T(1024)}, f32[768]{0:T(1024)}) all-reduce(f32[768]{0:T(1024)S(1)} %get-tuple-element.19, f32[768]{0:T(1024)S(1)} %get-tuple-element.17), channel_id=1, replica_groups=mesh['dp'=8,'mp'=4] {'dp','mp'}, use_global_device_ids=true, to_apply=%region_13.14 | all-reduce | flops 1536 | bytes 12288 | tf_op jit(solution)/shard_map/psum | solution.py:377
  624.3 3.0 add_add_fusion.2
  627.3 89.1 %all-reduce.8.cloned.1.call-done = (f32[768,3,192]{0,2,1:T(8,128)}, f32[192,2048]{1,0:T(8,128)}, f32[192,768]{1,0:T(8,128)}, f32[768,768]{1,0:T(8,128)}, f32[768,768]{1,0:T(8,128)}) async-done(((f32[768,3,192]{0,2,1:T(8,128)}, f32[192,2048]{1,0:T(8,128)}, f32[192,768]{1,0:T(8,128)}, f32[768,768]{1,0:T(8,128)}, f32[768,768]{1,0:T(8,128)}), (f32[768,3,192]{0,2,1:T(8,128)}, f32[192,2048]{1,0:T(8,128)}, ...) | async-done | bytes 8650768 | tf_op jit(solution)/shard_map/psum | solution.py:376
  716.5 2.9 copy.27
  (133 shorter events, 36.0 us)
Async XLA Ops:
  7.2 219.6 %copy-start = (bf16[768,768]{1,0:T(8,128)(2,1)S(1)}, bf16[768,768]{1,0:T(8,128)(2,1)}, u32[]{:S(2)}) copy-start(bf16[768,768]{1,0:T(8,128)(2,1)} %param.20) | copy-start | bytes 3538948
  7.2 4.3 copy-start.2
  7.2 4.3 copy-start.25
  7.2 71.9 %all-gather.5.cloned.1.call-start = ((), (), s32[]{:S(2)}) async-start(), calls=%async_computation.4 | async-start | bytes 3932160 | tf_op jit(solution)/shard_map/all_gather | solution.py:325
  8.7 4.1 copy-start.37
  8.7 4.1 copy-start.11
  12.7 147.1 %reduce-scatter.5.cloned.1.call-start = ((), (), s32[]{:S(2)}) async-start(), calls=%async_computation.5 | async-start | bytes 3932160 | tf_op jit(solution)/shard_map/reduce_scatter | solution.py:333
  15.5 63.6 %copy-start.41 = (bf16[768,3,192]{0,2,1:T(8,128)(2,1)S(1)}, bf16[768,3,192]{0,2,1:T(8,128)(2,1)}, u32[]{:S(2)}) copy-start(bf16[768,3,192]{0,2,1:T(8,128)(2,1)} %param.15) | copy-start | bytes 2654212
  95.1 3.0 copy-start.23
  100.8 61.0 %copy-start.26 = (f32[768]{0:T(1024)S(1)}, f32[768]{0:T(1024)}, u32[]{:S(2)}) copy-start(f32[768]{0:T(1024)} %param.19) | copy-start | bytes 9220
  100.8 125.9 %all-gather.7.cloned.1.call-start = ((), (), s32[]{:S(2)}) async-start(), calls=%async_computation.6 | async-start | bytes 3932160 | tf_op jit(solution)/shard_map/all_gather | solution.py:337
  163.1 127.3 %all-gather.9.cloned.1.call-start = ((), (), s32[]{:S(2)}) async-start(), calls=%async_computation.8 | async-start | bytes 3932160 | tf_op jit(solution)/shard_map/all_gather | solution.py:338
  163.6 199.9 %reduce-scatter.9.cloned.1.call-start = ((), (), s32[]{:S(2)}) async-start(), calls=%async_computation.9 | async-start | bytes 3932160 | tf_op jit(solution)/shard_map/reduce_scatter | solution.py:349
  304.5 121.5 %reduce-scatter.7.cloned.1.call-start = ((), (), s32[]{:S(2)}) async-start(), calls=%async_computation.7 | async-start | bytes 3932160 | tf_op jit(solution)/shard_map/reduce_scatter | solution.py:343
  314.0 49.5 %copy-start.30 = (f32[512]{0:T(512)S(1)}, f32[512]{0:T(512)}, u32[]{:S(2)}) copy-start(f32[512]{0:T(512)} %copy-done.29) | copy-start | bytes 6148
  314.0 51.6 %copy-start.34 = (f32[512]{0:T(512)S(1)}, f32[512]{0:T(512)}, u32[]{:S(2)}) copy-start(f32[512]{0:T(512)} %copy-done.33) | copy-start | bytes 6148
  314.0 180.8 %all-gather.11.cloned.1.call-start = ((), (), s32[]{:S(2)}) async-start(), calls=%async_computation.10 | async-start | bytes 3932160 | tf_op jit(solution)/shard_map/all_gather | solution.py:356
  363.6 62.5 %copy-start.13 = (bf16[1,512,768]{2,1,0:T(8,128)(2,1)S(1)}, bf16[1,512,768]{2,1,0:T(8,128)(2,1)}, u32[]{:S(2)}) copy-start(bf16[1,512,768]{2,1,0:T(8,128)(2,1)} %reduce-scatter.9.cloned.1.call-done) | copy-start | bytes 2359300
  365.7 64.3 %copy-start.10 = (bf16[1,512,768]{2,1,0:T(8,128)(2,1)S(1)}, bf16[1,512,768]{2,1,0:T(8,128)(2,1)}, u32[]{:S(2)}) copy-start(bf16[1,512,768]{2,1,0:T(8,128)(2,1)} %param.22) | copy-start | bytes 2359300
  430.0 64.9 %copy-start.8 = (f32[1,192,2048]{2,1,0:T(8,128)S(1)}, f32[1,192,2048]{2,1,0:T(8,128)}, u32[]{:S(2)}) copy-start(f32[1,192,2048]{2,1,0:T(8,128)} %get-tuple-element.13) | copy-start | bytes 4718596
  430.0 64.9 %copy-start.24 = (bf16[192,768]{1,0:T(8,128)(2,1)S(1)}, bf16[192,768]{1,0:T(8,128)(2,1)}, u32[]{:S(2)}) copy-start(bf16[192,768]{1,0:T(8,128)(2,1)} %param.18) | copy-start | bytes 884740
  431.2 147.8 %reduce-scatter.11.cloned.1.call-start = ((), (), s32[]{:S(2)}) async-start(), calls=%async_computation.11 | async-start | bytes 3932160 | tf_op jit(solution)/shard_map/reduce_scatter | solution.py:371
  497.9 17.9 %copy-start.18 = (bf16[1,192,2048]{2,1,0:T(8,128)(2,1)}, bf16[1,192,2048]{2,1,0:T(8,128)(2,1)S(1)}, u32[]{:S(2)}) copy-start(bf16[1,192,2048]{2,1,0:T(8,128)(2,1)S(1)} %get-tuple-element.33) | copy-start | bytes 2359300
  519.9 196.5 %all-reduce.8.cloned.1.call-start = ((), (), s32[]{:S(2)}) async-start(), calls=%async_computation.12 | async-start | bytes 17301504 | tf_op jit(solution)/shard_map/psum | solution.py:376
  520.2 7.1 copy-start.39
  527.3 7.6 %copy-start.3 = (bf16[1,2048,768]{2,1,0:T(8,128)(2,1)S(1)}, bf16[1,2048,768]{2,1,0:T(8,128)(2,1)}, u32[]{:S(2)}) copy-start(bf16[1,2048,768]{2,1,0:T(8,128)(2,1)} %all-gather.11.cloned.1.call-done) | copy-start | bytes 9437188
  527.3 7.6 %copy-start.15 = (bf16[192,2048]{1,0:T(8,128)(2,1)S(1)}, bf16[192,2048]{1,0:T(8,128)(2,1)}, u32[]{:S(2)}) copy-start(bf16[192,2048]{1,0:T(8,128)(2,1)} %copy-done.14) | copy-start | bytes 2359300
  544.0 36.7 %copy-start.32 = (f32[512]{0:T(512)S(1)}, f32[512]{0:T(512)}, u32[]{:S(2)}) copy-start(f32[512]{0:T(512)} %copy-done.31) | copy-start | bytes 6148
  544.0 36.7 %copy-start.28 = (f32[512]{0:T(512)S(1)}, f32[512]{0:T(512)}, u32[]{:S(2)}) copy-start(f32[512]{0:T(512)} %copy-done.27) | copy-start | bytes 6148
  544.0 80.3 %copy-start.7 = (f32[1,512,768]{2,1,0:T(8,128)S(1)}, f32[1,512,768]{2,1,0:T(8,128)}, u32[]{:S(2)}) copy-start(f32[1,512,768]{2,1,0:T(8,128)} %copy-done.6) | copy-start | bytes 4718596
  579.0 45.3 %copy-start.9 = (bf16[1,512,768]{2,1,0:T(8,128)(2,1)S(1)}, bf16[1,512,768]{2,1,0:T(8,128)(2,1)}, u32[]{:S(2)}) copy-start(bf16[1,512,768]{2,1,0:T(8,128)(2,1)} %reduce-scatter.11.cloned.1.call-done) | copy-start | bytes 2359300
  721.8 3.9 copy-start.1
  (21 other events, 34.8 us)
Sparse Core Ops, SparseCore 0:
  12.9 66.1 all-gather.4
  100.9 58.8 reduce-scatter.4
  163.2 63.5 all-gather.6
  228.2 62.1 all-gather.8
  304.6 58.8 reduce-scatter.8
  365.7 60.2 reduce-scatter.6
  431.3 63.5 all-gather.10
  520.1 58.8 reduce-scatter.10
  584.5 131.9 all-reduce.7
